TPU v7x, 32 devices: a whole 2x2x4 slice. The times are simulated.
32 devices in a mesh: tile: 8 (over z, y), chan: 4 (over x, core).
Axes of the slice: x: 2, y: 2, z: 4, core: 2. Of those that a mesh axis runs over, the one named last changes fastest.
Arguments:
- feat: bfloat16 [128, 64, 256], P('tile', 'chan'), may hold values from -6 to 6
- lift: float32 [64], replicated, may hold values from -3 to 3
- dilation4_weight: bfloat16 [3, 3, 64, 64], replicated, may hold values from -0.25 to 0.25
- dilation8_weight: bfloat16 [3, 3, 64, 64], replicated, may hold values from -0.25 to 0.25
- entry_fraction: bfloat16 [2048, 128], P('tile'), may hold values from 0.019897461 to 0.19921875
- entry_target_tile: int32 [2048, 1], P('tile'), may hold values from 0 to 7; in each aligned block of 256 rows (0 to 255, 256 to 511, ...) at most 64 rows name the same one
- entry_owner_tile: int32 [2048], P('tile'), may hold values from 0 to 31
- entry_local_net: int32 [2048], P('tile'), may hold values from 0 to 63
- pin_demand_weight: float32 [2048], P('tile'), may hold values from 0.2 to 2
- pin_local_net: int32 [2048], P('tile'), may hold values from 0 to 63
- pin_global_cell: int32 [2048], P('tile'), may hold values from 0 to 511
Outputs:
- cell_grad: float32 [512], P('tile')
Inputs may be any that keep to these rules, and one draw needn't show every extreme that they name: `entry_target_tile`: among the entries of one tile index, at most 64 name the same destination, and in some tile index exactly 64 do.
All inputs are finite; a program needn't handle non-finite values.
Results may differ from a plain program's by a relative error of at most 0.0003.
Values may be sent and summed in bfloat16 or wider, within the bound.
A program may use at most 64 MiB of HBM per device.

v0:
```python
import functools

import jax
import jax.numpy as jnp
from jax import lax
from jax.experimental import pallas as pl
from jax.experimental.pallas import tpu as pltpu
from jax.sharding import PartitionSpec as P

MESH = pl.DeviceIdType.MESH
CELL_DEV = 64
TILE_ROWS = 8
TILE_COLS = 16
LANES = 128
HALO = 24
GROUP = 4
F32 = jnp.float32
BF16 = jnp.bfloat16


def split(x, terms):
    parts = []
    for _ in range(terms):
        part = x.astype(BF16)
        parts.append(part)
        x = x - part.astype(F32)
    return parts


def kernel(
    tiles, chans,
    feat_in, lift_in, w4_in, w8_in, frac_in, target_in, owner_in, net_e_in, weight_in, net_p_in,
    cell_in,
    out,
    feat, lift, w4, w8, frac, target, owner, net_e, weight, net_p, cell, load_sem,
    win, gath, inp, pre, hid, sec, gpre, wm1, wm2, wm3, wm4,
    fmask, block_hot, same_net, by_dest, by_cell, dbuf, dsend, drecv, demand, gown, gall, csend, crecv,
    fsend_sem, frecv_sem, own_sem, dsend_sem, drecv_sem, gsend_sem, grecv_sem, gown_sem,
    csend_sem, crecv_sem,
):
    ti = lax.axis_index("tile")
    ci = lax.axis_index("chan")
    rows, chan_own, cols = feat.shape
    chan = chan_own * chans
    own_cols = cols // chans
    margin = (LANES - own_cols) // 2
    reach = -(-HALO // rows)
    in_rows = rows + 2 * HALO
    others = tiles * chans - 1

    loads = [
        pltpu.make_async_copy(src, dst, load_sem.at[n])
        for n, (src, dst) in enumerate(
            [
                (feat_in, feat), (target_in, target), (owner_in, owner), (net_e_in, net_e),
                (weight_in, weight), (net_p_in, net_p), (frac_in, frac), (lift_in, lift),
                (cell_in, cell), (w4_in, w4), (w8_in, w8),
            ]
        )
    ]
    for load in loads:
        load.start()

    barrier = pltpu.get_barrier_semaphore()

    def wrap(number, count):
        return jnp.where(number >= count, number - count, number)

    def each(lo, hi, fn):
        if hi - lo <= 32:
            for step in range(lo, hi):
                fn(step)
        else:
            def body(step, carry):
                fn(step)
                return carry
            lax.fori_loop(lo, hi, body, 0)

    def each_peer(fn):
        def along(back):
            hop = tiles - 1 - back
            for turn in range(chans):
                fn(hop * chans + turn, (wrap(ti + hop, tiles), wrap(ci + turn, chans)))
        each(0, tiles - 1, along)
        for turn in range(1, chans):
            fn(turn, (ti, wrap(ci + turn, chans)))

    each_peer(
        lambda n, who: pl.semaphore_signal(barrier, inc=1, device_id=who, device_id_type=MESH)
    )

    loads[0].wait()

    flat = feat[...].astype(F32).reshape(rows * chan_own, cols)
    lane = lax.broadcasted_iota(jnp.int32, (1, LANES), 1)
    for k in range(chans):
        first = k * own_cols - margin
        turned = pltpu.roll(flat, (-first) % cols, 1)[:, :LANES]
        inside = (lane + first >= 0) & (lane + first < cols)
        win[k] = jnp.where(inside, turned, 0.0).astype(BF16).reshape(rows, chan_own, LANES)

    def spans(delta):
        start = HALO - rows * delta
        low = max(0, -start)
        high = min(rows, in_rows - start)
        return low, high - low, start + low

    def feat_copy(delta, k):
        low, count, at = spans(delta)
        to = wrap(ci + k, chans)
        src = win.at[to, pl.ds(low, count)]
        dst = gath.at[pl.ds(at, count), pl.ds(pl.multiple_of(ci * chan_own, chan_own), chan_own)]
        if delta == 0 and k == 0:
            return pltpu.make_async_copy(src, dst, own_sem)
        return pltpu.make_async_remote_copy(
            src_ref=src, dst_ref=dst,
            send_sem=fsend_sem.at[delta + reach, k], recv_sem=frecv_sem.at[delta + reach, k],
            device_id=(ti + delta, to), device_id_type=MESH,
        )

    def feat_arrival(delta, k):
        low, count, at = spans(delta)
        come = wrap(ci + chans - k, chans)
        dst = gath.at[pl.ds(at, count), pl.ds(pl.multiple_of(come * chan_own, chan_own), chan_own)]
        return pltpu.make_async_remote_copy(
            src_ref=dst, dst_ref=dst,
            send_sem=fsend_sem.at[delta + reach, k], recv_sem=frecv_sem.at[delta + reach, k],
            device_id=(ti, wrap(ci + 1, chans)), device_id_type=MESH,
        )

    stages = [[0]] + [[d] if abs(d) == 1 else [d, -d] for d in (1, -1, *range(2, reach + 1))]
    for delta in sum(stages[1:], []):
        @pl.when((ti - delta < 0) | (ti - delta >= tiles))
        def _(delta=delta):
            low, count, at = spans(delta)
            gath[at : at + count] = jnp.zeros((count, chan, LANES), BF16)

    for load in loads[1:]:
        load.wait()
    per_row = cols // TILE_COLS
    own, cell_no = owner[...], cell[...]
    table = jnp.concatenate(
        [
            (target[...] * (rows // TILE_ROWS) + own // per_row).astype(F32),
            (own % per_row).astype(F32),
            net_e[...].astype(F32),
            weight[...],
            net_p[...].astype(F32),
            (cell_no // CELL_DEV).astype(F32),
            (cell_no % CELL_DEV).astype(F32),
            jnp.zeros_like(weight[...]),
        ],
        axis=0,
    )
    columns = jnp.transpose(table)
    entries = table.shape[1]
    net_e_col, wpin_col, net_p_col = columns[:, 2:3], columns[:, 3:4], columns[:, 4:5]
    strength = jnp.sum(
        jnp.where(net_p_col == table[2:3, :], wpin_col, 0.0), axis=0, keepdims=True
    )
    src_j = lax.broadcasted_iota(jnp.int32, (LANES, TILE_ROWS * LANES), 0)
    dst_j = lax.broadcasted_iota(jnp.int32, (LANES, TILE_ROWS * LANES), 1)
    pick = src_j == (dst_j // LANES) * TILE_COLS + dst_j % TILE_COLS
    spread = jnp.dot(
        frac[...], jnp.where(pick, 1.0, 0.0).astype(BF16), preferred_element_type=F32
    )
    wide = lax.broadcasted_iota(jnp.int32, (1, TILE_ROWS * LANES), 1) % LANES
    block = (wide + ci * own_cols - margin + TILE_COLS * LANES) // TILE_COLS - LANES
    fmask[...] = jnp.where(columns[:, 1:2] == block.astype(F32), spread, 0.0).astype(BF16)
    pad_blocks = HALO // TILE_ROWS
    blocks = dbuf.shape[0] // TILE_ROWS
    block_row = lax.broadcasted_iota(jnp.int32, (blocks, entries), 0).astype(F32)
    placed = jnp.where(block_row == table[0:1, :] + float(pad_blocks), strength, 0.0)
    left = jnp.concatenate(split(placed, 2), axis=0)
    partial = jnp.dot(left, fmask[...], preferred_element_type=F32)
    partial = partial[:blocks] + partial[blocks:]
    for i in range(TILE_ROWS):
        dbuf[pl.ds(i, blocks, stride=TILE_ROWS), :] = partial[:, i * LANES : (i + 1) * LANES]
    dsend[...] = dbuf[...].astype(BF16)

    def demand_copy(step):
        to = wrap(ti + step, tiles)
        return pltpu.make_async_remote_copy(
            src_ref=dsend.at[pl.ds(pl.multiple_of(to * rows, rows), in_rows)],
            dst_ref=drecv.at[step],
            send_sem=dsend_sem.at[step], recv_sem=drecv_sem.at[step],
            device_id=(to, ci), device_id_type=MESH,
        )

    lift_row = lift[...]
    lift_col = jnp.transpose(jnp.broadcast_to(lift_row, (LANES, chan)))
    for u in range(3):
        for v in range(3):
            at_v, at_u = slice(v * chan, (v + 1) * chan), slice(u * chan, (u + 1) * chan)
            wm1[at_v, at_u] = jnp.transpose(w4[u, v].astype(F32)).astype(BF16)
            wm2[at_v, at_u] = jnp.transpose(w8[u, v].astype(F32)).astype(BF16)
            wm3[at_v, at_u] = w8[2 - u, 2 - v]
    taps = []
    for v in range(3):
        taps.append(
            jnp.concatenate(
                [
                    jnp.sum(
                        w4[2 - u, 2 - v].astype(F32) * lift_col[:, :chan], axis=0, keepdims=True
                    )
                    for u in range(3)
                ],
                axis=1,
            )
        )
    tap_rows = jnp.concatenate(taps + [jnp.zeros((5, 3 * chan), F32)], axis=0)
    hi, mid, low_part = [p.astype(F32) for p in split(tap_rows, 3)]
    wm4[...] = jnp.concatenate(
        [hi, mid, low_part, jnp.zeros((8, 3 * chan), F32)], axis=0
    ).astype(BF16)

    map_blocks = rows * tiles // TILE_ROWS
    block_lane = lax.broadcasted_iota(jnp.int32, (entries, map_blocks), 1).astype(F32)
    block_hot[...] = jnp.where(columns[:, 0:1] == block_lane, 1.0, 0.0).astype(BF16)
    same_net[...] = jnp.where(net_e_col == table[4:5, :], 1.0, 0.0)
    dest_rows = max(8, tiles)
    dest_row = lax.broadcasted_iota(jnp.int32, (dest_rows, entries), 0).astype(F32)
    cell_row = lax.broadcasted_iota(jnp.int32, (LANES, entries), 0).astype(F32)
    by_dest[...] = jnp.where(dest_row == table[5:6, :], 1.0, 0.0)
    by_cell[...] = jnp.where(cell_row == table[6:7, :], 1.0, 0.0).astype(BF16)

    pl.semaphore_wait(barrier, others)

    each(1, tiles, lambda s: demand_copy(s).start())

    for delta in sum(stages, []):
        for k in range(chans):
            if delta == 0:
                feat_copy(delta, k).start()
            else:
                @pl.when((ti + delta >= 0) & (ti + delta < tiles))
                def _(delta=delta, k=k):
                    feat_copy(delta, k).start()

    each(1, tiles, lambda s: demand_copy(s).wait())
    total = dsend[pl.ds(pl.multiple_of(ti * rows, rows), in_rows), :].astype(F32)
    total = lax.fori_loop(1, tiles, lambda s, t: t + drecv[s].astype(F32), total)
    demand[...] = total

    def feat_wait(delta):
        if delta == 0:
            feat_copy(delta, 0).wait()
            for k in range(1, chans):
                feat_arrival(delta, k).wait_recv()
        else:
            @pl.when((ti - delta >= 0) & (ti - delta < tiles))
            def _():
                for k in range(chans):
                    feat_arrival(delta, k).wait_recv()

    height = rows * tiles
    top = ti * rows

    def in_map(row):
        return (row >= 0) & (row < height)

    def fill(at):
        for j in range(at, at + GROUP):
            add = lift_col * demand[j : j + 1, :]
            inp[j] = (gath[j].astype(F32) + add).astype(BF16)

    col = lane + ci * own_cols - margin
    col_ok = ((col >= 0) & (col < cols)).astype(F32)

    def gathered(ref, at, dilation):
        return jnp.concatenate(
            [
                jnp.concatenate([ref[at + j + u * dilation] for u in range(3)], axis=0)
                for j in range(GROUP)
            ],
            axis=1,
        )

    def conv(ref, at, weights, dilation):
        result = jnp.dot(weights[...], gathered(ref, at, dilation), preferred_element_type=F32)
        parts = []
        for j in range(GROUP):
            one = result[:, j * LANES : (j + 1) * LANES]
            parts.append(
                one[chan : 2 * chan]
                + pltpu.roll(one[:chan], dilation, 1)
                + pltpu.roll(one[2 * chan :], LANES - dilation, 1)
            )
        return parts

    def keep_of(row):
        return col_ok * in_map(row).astype(F32)

    def first(at):
        keep = keep_of(top - 20 + at)
        for j, value in enumerate(conv(inp, at, wm1, 4)):
            pre[at + j] = value
            hid[at + j] = (value * jax.nn.sigmoid(value) * keep).astype(BF16)

    def second(at):
        keep = keep_of(top - 12 + at)
        for j, value in enumerate(conv(hid, at, wm2, 8)):
            sec[at + j] = (jax.nn.sigmoid(value) * keep).astype(BF16)

    def third(at):
        keep = keep_of(top - 4 + at)
        for j, value in enumerate(conv(sec, at, wm3, 8)):
            p = pre[at + j + 16]
            s = jax.nn.sigmoid(p)
            gpre[at + j] = (value * s * (1.0 + p * (1.0 - s)) * keep).astype(BF16)

    here, done = set(), set()
    for stage in stages:
        fresh = set()
        for delta in stage:
            feat_wait(delta)
            low, count, at = spans(delta)
            fresh |= set(range(at, at + count))
        here |= fresh
        for at in range(0, in_rows, GROUP):
            if at in fresh:
                fill(at)
        for at in range(0, rows + 40, GROUP):
            if at not in done and all(at + j in here for j in range(GROUP + 8)):
                done.add(at)
                first(at)
    for at in range(0, rows + 24, GROUP):
        second(at)
    for at in range(0, rows + 8, GROUP):
        third(at)

    owned = ((lane >= margin) & (lane < margin + own_cols)).astype(F32)
    for g in range(rows // GROUP):
        at = g * GROUP
        result = jnp.dot(wm4[...], gathered(gpre, at, 4), preferred_element_type=F32)
        result = result[0:8] + result[8:16] + result[16:24]
        for j in range(GROUP):
            one = result[:, j * LANES : (j + 1) * LANES]
            line = (
                one[1:2]
                + pltpu.roll(one, 4, 1)[0:1]
                + pltpu.roll(one, LANES - 4, 1)[2:3]
            )
            gown[at + j : at + j + 1, :] = line * owned

    def grad_copy(step):
        to = wrap(ti + step, tiles)
        return pltpu.make_async_remote_copy(
            src_ref=gown, dst_ref=gall.at[pl.ds(pl.multiple_of(ti * rows, rows), rows)],
            send_sem=gsend_sem.at[step], recv_sem=grecv_sem.at[step],
            device_id=(to, ci), device_id_type=MESH,
        )

    def grad_arrival(step):
        come = wrap(ti + tiles - step, tiles)
        dst = gall.at[pl.ds(pl.multiple_of(come * rows, rows), rows)]
        return pltpu.make_async_remote_copy(
            src_ref=gown, dst_ref=dst,
            send_sem=gsend_sem.at[step], recv_sem=grecv_sem.at[step],
            device_id=(wrap(ti + step, tiles), ci), device_id_type=MESH,
        )

    each(1, tiles, lambda s: grad_copy(s).start())
    mine = pltpu.make_async_copy(
        gown, gall.at[pl.ds(pl.multiple_of(ti * rows, rows), rows)], gown_sem
    )
    mine.start()
    mine.wait()
    each(1, tiles, lambda s: grad_arrival(s).wait_recv())

    entry_sum = jnp.zeros((entries, LANES), F32)
    for i in range(TILE_ROWS):
        grads = gall[pl.ds(i, map_blocks, stride=TILE_ROWS), :]
        high, low_ = split(grads, 2)
        rows_of = jnp.dot(block_hot[...], high, preferred_element_type=F32)
        rows_of = rows_of + jnp.dot(block_hot[...], low_, preferred_element_type=F32)
        entry_sum = entry_sum + rows_of * fmask[:, i * LANES : (i + 1) * LANES].astype(F32)
    entry_grad = jnp.sum(entry_sum, axis=1, keepdims=True)
    pin_grad = jnp.sum(same_net[...] * entry_grad, axis=0, keepdims=True)
    pieces = jnp.concatenate([p.astype(F32) for p in split(by_dest[...] * pin_grad, 3)], axis=0).astype(BF16)
    cells = lax.dot_general(
        pieces, by_cell[...], (((1,), (1,)), ((), ())), preferred_element_type=F32
    )
    cells = cells[:dest_rows] + cells[dest_rows : 2 * dest_rows] + cells[2 * dest_rows :]
    for t in range(tiles):
        csend[t] = cells[t : t + 1, :]

    def cell_copy(step, to):
        return pltpu.make_async_remote_copy(
            src_ref=csend.at[to[0]], dst_ref=crecv.at[step],
            send_sem=csend_sem, recv_sem=crecv_sem,
            device_id=to, device_id_type=MESH,
        )

    each_peer(lambda n, who: cell_copy(n, who).start())

    for delta in sum(stages, []):
        for k in range(chans):
            if delta == 0:
                if k:
                    feat_copy(delta, k).wait_send()
            else:
                @pl.when((ti + delta >= 0) & (ti + delta < tiles))
                def _(delta=delta, k=k):
                    feat_copy(delta, k).wait_send()
    each(1, tiles, lambda s: grad_copy(s).wait_send())
    arrived = crecv.at[pl.ds(1, others)]
    pltpu.make_async_remote_copy(
        src_ref=arrived, dst_ref=arrived, send_sem=csend_sem, recv_sem=crecv_sem,
        device_id=(ti, wrap(ci + 1, chans)), device_id_type=MESH,
    ).wait()
    out[...] = csend[ti] + jnp.sum(crecv[1:], axis=0)


def solution(mesh):
    tiles, chans = mesh.shape["tile"], mesh.shape["chan"]

    def local(
        feat, lift, w4, w8, frac, target, owner, net_e, weight, net_p, cell,
    ):
        rows, chan_own, cols = feat.shape
        chan = chan_own * chans
        entries = frac.shape[0]
        pins = weight.shape[0]
        in_rows = rows + 2 * HALO
        reach = -(-HALO // rows)
        height = rows * tiles
        blocks = -(-(height + 2 * HALO) // (8 * TILE_ROWS)) * 8
        vm = pltpu.VMEM
        dma = pltpu.SemaphoreType.DMA
        result = pl.pallas_call(
            functools.partial(kernel, tiles, chans),
            out_shape=jax.ShapeDtypeStruct((1, LANES), F32),
            in_specs=[pl.BlockSpec(memory_space=pltpu.HBM)] * 11,
            out_specs=pl.BlockSpec(memory_space=pltpu.VMEM),
            scratch_shapes=[
                vm(feat.shape, BF16),
                vm((1, chan), F32),
                vm(w4.shape, BF16),
                vm(w8.shape, BF16),
                vm(frac.shape, BF16),
                vm((1, entries), jnp.int32),
                vm((1, entries), jnp.int32),
                vm((1, entries), jnp.int32),
                vm((1, pins), F32),
                vm((1, pins), jnp.int32),
                vm((1, pins), jnp.int32),
                dma((11,)),
                vm((chans, rows, chan_own, LANES), BF16),
                vm((in_rows, chan, LANES), BF16),
                vm((in_rows, chan, LANES), BF16),
                vm((rows + 40, chan, LANES), F32),
                vm((rows + 40, chan, LANES), BF16),
                vm((rows + 24, chan, LANES), BF16),
                vm((rows + 8, chan, LANES), BF16),
                vm((3 * chan, 3 * chan), BF16),
                vm((3 * chan, 3 * chan), BF16),
                vm((3 * chan, 3 * chan), BF16),
                vm((32, 3 * chan), BF16),
                vm((entries, TILE_ROWS * LANES), BF16),
                vm((entries, height // TILE_ROWS), BF16),
                vm((entries, pins), F32),
                vm((max(8, tiles), pins), F32),
                vm((LANES, pins), BF16),
                vm((blocks * TILE_ROWS, LANES), F32),
                vm((blocks * TILE_ROWS, LANES), BF16),
                vm((tiles, in_rows, LANES), BF16),
                vm((in_rows, LANES), F32),
                vm((rows, LANES), F32),
                vm((height, LANES), F32),
                vm((tiles, 1, LANES), F32),
                vm((tiles * chans, 1, LANES), F32),
                dma((2 * reach + 1, chans)),
                dma((2 * reach + 1, chans)),
                dma(()),
                dma((tiles,)),
                dma((tiles,)),
                dma((tiles,)),
                dma((tiles,)),
                dma(()),
                dma(()),
                dma(()),
            ],
            compiler_params=pltpu.CompilerParams(collective_id=0, has_side_effects=True),
        )(
            feat, lift.reshape(1, chan), w4, w8, frac, target.reshape(1, entries),
            owner.reshape(1, entries), net_e.reshape(1, entries), weight.reshape(1, pins),
            net_p.reshape(1, pins), cell.reshape(1, pins),
        )
        return result[0, :CELL_DEV]

    in_specs = (
        P("tile", "chan", None), P(), P(), P(),
        P("tile", None), P("tile", None),
        P("tile"), P("tile"), P("tile"), P("tile"), P("tile"),
    )
    return jax.shard_map(
        local, mesh=mesh, in_specs=in_specs, out_specs=P("tile"), check_vma=False
    )
```

profile of v0, /device:TPU:0, one launch (start us, length us, event | category | flops | bytes accessed | tf_op | source)
XLA Modules:
  0.0 35.9 jit_solution(2307954516210022291)
XLA Ops:
  0.0 34.7 %shard_map.109 = f32[1,128]{1,0:T(1,128)} custom-call(bf16[16,16,256]{2,1,0:T(8,128)(2,1)} %feat_in.1, f32[1,64]{1,0:T(1,128)} %bitcast.15, bf16[3,3,64,64]{3,2,1,0:T(8,128)(2,1)} %w4_in.1, bf16[3,3,64,64]{3,2,1,0:T(8,128)(2,1)} %w8_in.1, bf16[256,128]{1,0:T(8,128)(2,1)} %frac_in.1, s32[1,256]{1,0:T(1,128)} %bitcast.9, s32[1,256]{1,0:T(1,128)} %bitcast.10, ...), custom_call_target="tpu_custom_call" | custom-call | tf_op jit(solution)/shard_map/pallas_call | solution.py:431
  34.7 1.2 %slice_bitcast_fusion = f32[64]{0:T(128)} fusion(f32[1,128]{1,0:T(1,128)} %shard_map.109), kind=kLoop, calls=%fused_computation | loop fusion | bytes 512 | tf_op jit(solution)/shard_map/squeeze | solution.py:490
where the time goes:
time: 36 us; the launch traced here: 35.9 us
  Pallas kernels  34.7 us (96%)
  local copies, waits for them, and re-layouts  1.19 us (3%)
    pallas_call x1, Pallas kernels, local(): pl.pallas_call(functools.partial(kernel, tiles, chans), out_shape=jax.Sha...  34.7 us
    squeeze x1, local copies, waits for them, and re-layouts, local(): return result[0, :CELL_DEV]  1.19 us

commit v1 on v0

v1 whole, which is shorter than its diff:
```python
import functools

import jax
import jax.numpy as jnp
from jax import lax
from jax.experimental import pallas as pl
from jax.experimental.pallas import tpu as pltpu
from jax.sharding import PartitionSpec as P

MESH = pl.DeviceIdType.MESH
CELL_DEV = 64
TILE_ROWS = 8
TILE_COLS = 16
LANES = 128
HALO = 24
GROUP = 4
META = 16
SPREAD = 4096
RIMS = ("A0", "B0", "F", "A1", "B1", "R")
F32 = jnp.float32
BF16 = jnp.bfloat16


def split(x, terms):
    parts = []
    for _ in range(terms):
        part = x.astype(BF16)
        parts.append(part)
        x = x - part.astype(F32)
    return parts


def kernel(
    tiles, chans,
    feat_in, lift_in, w4_in, w8_in, frac_in, target_in, owner_in, net_e_in, weight_in, net_p_in,
    cell_in,
    out,
    feat, lift, w4, w8, frac, target, owner, net_e, weight, net_p, cell, load_sem,
    win, gath, inp, pre, hid, sec, gpre, wm1, wm2, wm3, wm4,
    fmask, dbuf, dsend, drecv, demand, gown, esend, erecv, to_cell, tile_hot, csend, crecv,
    fsend_sem, frecv_sem, own_sem, hsend_sem, hrecv_sem, dsend_sem, drecv_sem,
    esend_sem, erecv_sem, csend_sem, crecv_sem,
):
    ti = lax.axis_index("tile")
    ci = lax.axis_index("chan")
    rows, chan_own, cols = feat.shape
    chan = chan_own * chans
    own_cols = cols // chans
    margin = (LANES - own_cols) // 2
    half = rows // 2
    in_rows = rows + 2 * HALO
    others = tiles * chans - 1
    entries, pins = frac.shape[0], weight.shape[1]
    cap = esend.shape[1] - META
    per = LANES // cap
    height = rows * tiles

    par = ci % 2
    alike = ti % 2 == par
    wt = ti - ti % 2 + par
    wc = ci - par + ti % 2
    near = 2 * par - 1
    top = wt * rows

    def at_work(t, c):
        return (t - t % 2 + c % 2, c - c % 2 + t % 2)

    loads = [
        pltpu.make_async_copy(src, dst, load_sem.at[n])
        for n, (src, dst) in enumerate(
            [
                (feat_in, feat), (target_in, target), (owner_in, owner), (net_e_in, net_e),
                (weight_in, weight), (net_p_in, net_p), (frac_in, frac), (lift_in, lift),
                (cell_in, cell), (w4_in, w4), (w8_in, w8),
            ]
        )
    ]
    for load in loads:
        load.start()

    barrier = pltpu.get_barrier_semaphore()

    def wrap(number, count):
        return jnp.where(number >= count, number - count, number)

    def inside(strip):
        return (strip >= 0) & (strip < tiles)

    def each(lo, hi, fn):
        if hi - lo <= 32:
            for step in range(lo, hi):
                fn(step)
        else:
            def body(step, carry):
                fn(step)
                return carry
            lax.fori_loop(lo, hi, body, 0)

    def each_peer(fn):
        def along(back):
            hop = tiles - 1 - back
            for turn in range(chans):
                fn(hop * chans + turn, (wrap(ti + hop, tiles), wrap(ci + turn, chans)))
        each(0, tiles - 1, along)
        for turn in range(1, chans):
            fn(turn, (ti, wrap(ci + turn, chans)))

    each_peer(
        lambda n, who: pl.semaphore_signal(barrier, inc=1, device_id=who, device_id_type=MESH)
    )

    loads[0].wait()

    flat = feat[...].astype(F32).reshape(rows * chan_own, cols)
    lane = lax.broadcasted_iota(jnp.int32, (1, LANES), 1)
    for k in range(chans):
        first_col = k * own_cols - margin
        turned = pltpu.roll(flat, (-first_col) % cols, 1)[:, :LANES]
        on_map = (lane + first_col >= 0) & (lane + first_col < cols)
        win[k] = jnp.where(on_map, turned, 0.0).astype(BF16).reshape(rows, chan_own, LANES)

    def span(delta):
        low = max(0, rows * delta - HALO)
        high = min(rows, rows * delta + HALO + rows)
        return low, high - low, HALO - rows * delta + low

    for delta in (1, -1, 2, -2):
        @pl.when(jnp.logical_not(inside(wt - delta)))
        def _(delta=delta):
            _, count, at = span(delta)
            inp[at : at + count] = jnp.zeros((count, chan, LANES), BF16)

    for load in loads[1:]:
        load.wait()
    per_row = cols // TILE_COLS
    own, cell_no = owner[...], cell[...]
    target_row = target[...].astype(F32)
    table = jnp.concatenate(
        [
            (target[...] * (rows // TILE_ROWS) + own // per_row).astype(F32),
            (own % per_row).astype(F32),
            net_e[...].astype(F32),
            weight[...],
            net_p[...].astype(F32),
            target_row,
            jnp.zeros((2, entries), F32),
        ],
        axis=0,
    )
    columns = jnp.transpose(table)
    wpin_col, net_p_col = columns[:, 3:4], columns[:, 4:5]
    strength = jnp.sum(
        jnp.where(net_p_col == table[2:3, :], wpin_col, 0.0), axis=0, keepdims=True
    )
    src_j = lax.broadcasted_iota(jnp.int32, (LANES, TILE_ROWS * LANES), 0)
    dst_j = lax.broadcasted_iota(jnp.int32, (LANES, TILE_ROWS * LANES), 1)
    pick = src_j == (dst_j // LANES) * TILE_COLS + dst_j % TILE_COLS
    spread = jnp.dot(
        frac[...], jnp.where(pick, 1.0, 0.0).astype(BF16), preferred_element_type=F32
    )
    wide = lax.broadcasted_iota(jnp.int32, (1, TILE_ROWS * LANES), 1) % LANES
    block = (wide + ci * own_cols - margin + TILE_COLS * LANES) // TILE_COLS - LANES
    fmask[...] = jnp.where(columns[:, 1:2] == block.astype(F32), spread, 0.0).astype(BF16)
    blocks = height // TILE_ROWS
    block_row = lax.broadcasted_iota(jnp.int32, (blocks, entries), 0).astype(F32)
    placed = jnp.where(block_row == table[0:1, :], strength, 0.0)
    left = jnp.concatenate(split(placed, 2), axis=0)
    partial = jnp.dot(left, fmask[...], preferred_element_type=F32)
    partial = partial[:blocks] + partial[blocks:]
    for i in range(TILE_ROWS):
        dbuf[pl.ds(i, blocks, stride=TILE_ROWS), :] = partial[:, i * LANES : (i + 1) * LANES]
    dsend[...] = dbuf[...].astype(BF16)

    lift_row = lift[...]
    lift_col = jnp.transpose(jnp.broadcast_to(lift_row, (LANES, chan)))
    for u in range(3):
        for v in range(3):
            at_v, at_u = slice(v * chan, (v + 1) * chan), slice(u * chan, (u + 1) * chan)
            wm1[at_v, at_u] = jnp.transpose(w4[u, v].astype(F32)).astype(BF16)
            wm2[at_v, at_u] = jnp.transpose(w8[u, v].astype(F32)).astype(BF16)
            wm3[at_v, at_u] = w8[2 - u, 2 - v]
    taps = []
    for v in range(3):
        taps.append(
            jnp.concatenate(
                [
                    jnp.sum(
                        w4[2 - u, 2 - v].astype(F32) * lift_col[:, :chan], axis=0, keepdims=True
                    )
                    for u in range(3)
                ],
                axis=1,
            )
        )
    tap_rows = jnp.concatenate(taps + [jnp.zeros((5, 3 * chan), F32)], axis=0)
    hi, mid, low_part = [p.astype(F32) for p in split(tap_rows, 3)]
    wm4[...] = jnp.concatenate(
        [hi, mid, low_part, jnp.zeros((8, 3 * chan), F32)], axis=0
    ).astype(BF16)

    def feat_copy(turn, q, mine=False):
        h = ti % 2 if q == 0 else 1 - ti % 2
        to = wrap(ci + turn, chans)
        src = win.at[to, pl.ds(h * half, half)]
        dst = gath.at[
            pl.ds(h * half, half), pl.ds(pl.multiple_of(ci * chan_own, chan_own), chan_own)
        ]
        if mine:
            return pltpu.make_async_copy(src, dst, own_sem.at[q])
        return pltpu.make_async_remote_copy(
            src_ref=src, dst_ref=dst,
            send_sem=fsend_sem.at[q, turn], recv_sem=frecv_sem.at[q, turn],
            device_id=at_work(ti, to), device_id_type=MESH,
        )

    def feat_arrival(turn, q):
        h = par if q == 0 else 1 - par
        come = wrap(wc + chans - turn, chans)
        dst = gath.at[
            pl.ds(h * half, half), pl.ds(pl.multiple_of(come * chan_own, chan_own), chan_own)
        ]
        return pltpu.make_async_remote_copy(
            src_ref=dst, dst_ref=dst,
            send_sem=fsend_sem.at[q, turn], recv_sem=frecv_sem.at[q, turn],
            device_id=(ti, wrap(ci + 1, chans)), device_id_type=MESH,
        )

    def unless_mine(fn):
        @pl.when(jnp.logical_not(alike))
        def _():
            fn(False)

        @pl.when(alike)
        def _():
            fn(True)

    def feat_send(turn, q):
        if turn:
            feat_copy(turn, q).start()
        else:
            unless_mine(lambda mine: feat_copy(0, q, mine).start())

    def feat_wait(q):
        for turn in range(chans):
            if turn:
                feat_arrival(turn, q).wait_recv()
            else:
                unless_mine(
                    lambda mine: feat_copy(0, q, True).wait()
                    if mine else feat_arrival(0, q).wait_recv()
                )

    def demand_copy(step, mine=False):
        to = wrap(ti + step, tiles)
        src = dsend.at[pl.ds(pl.multiple_of(to * rows, rows), rows)]
        if mine:
            return pltpu.make_async_copy(src, drecv.at[step], own_sem.at[2])
        return pltpu.make_async_remote_copy(
            src_ref=src, dst_ref=drecv.at[step],
            send_sem=dsend_sem.at[step], recv_sem=drecv_sem.at[step],
            device_id=at_work(to, ci), device_id_type=MESH,
        )

    def entry_copy(step, mine=False):
        to = wrap(ti + step, tiles)
        if mine:
            return pltpu.make_async_copy(esend.at[to], erecv.at[ti], own_sem.at[3])
        return pltpu.make_async_remote_copy(
            src_ref=esend.at[to], dst_ref=erecv.at[ti],
            send_sem=esend_sem.at[step], recv_sem=erecv_sem.at[step],
            device_id=at_work(to, ci), device_id_type=MESH,
        )

    def entry_arrival(step):
        dst = erecv.at[wrap(wt + tiles - step, tiles)]
        return pltpu.make_async_remote_copy(
            src_ref=dst, dst_ref=dst,
            send_sem=esend_sem.at[step], recv_sem=erecv_sem.at[step],
            device_id=(ti, wrap(ci + 1, chans)), device_id_type=MESH,
        )

    pl.semaphore_wait(barrier, others)
    each(1, tiles, lambda s: demand_copy(s).start())
    unless_mine(lambda mine: demand_copy(0, mine).start())
    for q in range(2):
        for turn in range(chans - 1, -1, -1):
            feat_send(turn, q)

    before = lax.broadcasted_iota(jnp.int32, (entries, entries), 0) < lax.broadcasted_iota(
        jnp.int32, (entries, entries), 1
    )
    rank = jnp.sum(
        jnp.where((columns[:, 5:6] == target_row) & before, 1.0, 0.0), axis=0, keepdims=True
    )
    key = target_row * float(cap) + rank
    pin_rows = [
        row[:, n * LANES : (n + 1) * LANES]
        for row in (table[4:5, :], (cell_no // LANES).astype(F32), (cell_no % LANES).astype(F32))
        for n in range(pins // LANES)
    ]
    fixed = jnp.concatenate(
        [jnp.zeros((2, LANES), F32)] + pin_rows
        + [jnp.zeros((META - 2 - len(pin_rows), LANES), F32)],
        axis=0,
    )
    loose = jnp.concatenate(
        [table[2:3, :], own.astype(F32), jnp.zeros((META - 2, entries), F32)], axis=0
    ).astype(BF16)
    slot = lax.broadcasted_iota(jnp.int32, (cap, entries), 0).astype(F32)
    wide_slot = lax.broadcasted_iota(jnp.int32, (LANES, entries), 0) - (ti % per) * cap
    wide_slot = jnp.where(
        (wide_slot >= 0) & (wide_slot < cap), wide_slot, -(cap * tiles + 1)
    ).astype(F32)

    def pack(to):
        base = jnp.asarray(to * cap, F32) if isinstance(to, int) else (to * cap).astype(F32)
        hot = jnp.where(slot + base == key, 1.0, 0.0).astype(BF16)
        esend[to, :cap] = jnp.dot(hot, frac[...], preferred_element_type=F32).astype(BF16)
        hot = jnp.where(wide_slot + base == key, 1.0, 0.0).astype(BF16)
        meta = lax.dot_general(
            loose, hot, (((1,), (1,)), ((), ())), preferred_element_type=F32
        )
        esend[to, cap:] = (meta + fixed).astype(BF16)

    each(0, tiles, pack)
    each(1, tiles, lambda s: entry_copy(s).start())
    unless_mine(lambda mine: entry_copy(0, mine).start())

    def rim(role, sending):
        if role == "A0":
            to, h = wt + near, par
        elif role == "A1":
            to, h = wt + near, 1 - par
        elif role == "B0":
            to, h = wt - near, par
        elif role == "B1":
            to, h = wt - near, 1 - par
        else:
            to, h = wt - 2 * near, 1 - par
        n = RIMS.index(role)
        if sending:
            start = HALO + h * half
            if role == "R":
                start, to = HALO + rows * near + half * (1 - par), wt - near
                at = HALO + 2 * rows * near + half * (1 - par)
                there = inside(to) & inside(wt + near)
            else:
                at = HALO + (wt - to) * rows + h * half
                there = inside(to)
            copy = pltpu.make_async_remote_copy(
                src_ref=inp.at[pl.ds(start, half)], dst_ref=inp.at[pl.ds(at, half)],
                send_sem=hsend_sem.at[n], recv_sem=hrecv_sem.at[n],
                device_id=at_work(to, wc), device_id_type=MESH,
            )
        else:
            come, at = {
                "A0": (wt + near, HALO + rows * near + half * (1 - par)),
                "A1": (wt + near, HALO + rows * near + half * par),
                "B0": (wt - near, HALO - rows * near + half * (1 - par)),
                "B1": (wt - near, HALO - rows * near + half * par),
                "F": (wt + 2 * near, HALO + 2 * rows * near + half * (1 - par)),
                "R": (wt - 2 * near, HALO - 2 * rows * near + half * par),
            }[role]
            there = inside(come)
            dst = inp.at[pl.ds(at, half)]
            copy = pltpu.make_async_remote_copy(
                src_ref=dst, dst_ref=dst,
                send_sem=hsend_sem.at[n], recv_sem=hrecv_sem.at[n],
                device_id=(ti, wrap(ci + 1, chans)), device_id_type=MESH,
            )
        return there, copy

    def rim_start(role):
        there, copy = rim(role, True)

        @pl.when(there)
        def _():
            copy.start()

    def rim_sent(role):
        there, copy = rim(role, True)

        @pl.when(there)
        def _():
            copy.wait_send()

    def rim_wait(role):
        there, copy = rim(role, False)

        @pl.when(there)
        def _():
            copy.wait_recv()

    each(1, tiles, lambda s: demand_copy(s).wait())
    unless_mine(lambda mine: demand_copy(0, mine).wait())
    demand[...] = lax.fori_loop(
        1, tiles, lambda s, t: t + drecv[s].astype(F32), drecv[0].astype(F32)
    )

    def fill(h):
        for j in range(half):
            row = h * half + j
            add = lift_col * demand[pl.ds(row, 1), :]
            inp[HALO + row] = (gath[row].astype(F32) + add).astype(BF16)

    feat_wait(0)
    fill(par)
    rim_start("A0")
    rim_start("B0")
    feat_wait(1)
    fill(1 - par)
    rim_start("F")
    rim_start("A1")
    rim_start("B1")

    def in_map(row):
        return (row >= 0) & (row < height)

    col = lane + wc * own_cols - margin
    col_ok = ((col >= 0) & (col < cols)).astype(F32)

    def gathered(ref, at, dilation):
        return jnp.concatenate(
            [
                jnp.concatenate([ref[at + j + u * dilation] for u in range(3)], axis=0)
                for j in range(GROUP)
            ],
            axis=1,
        )

    def conv(ref, at, weights, dilation):
        result = jnp.dot(weights[...], gathered(ref, at, dilation), preferred_element_type=F32)
        parts = []
        for j in range(GROUP):
            one = result[:, j * LANES : (j + 1) * LANES]
            parts.append(
                one[chan : 2 * chan]
                + pltpu.roll(one[:chan], dilation, 1)
                + pltpu.roll(one[2 * chan :], LANES - dilation, 1)
            )
        return parts

    def keep_of(row):
        return col_ok * in_map(row).astype(F32)

    def first(at):
        keep = keep_of(top - 20 + at)
        for j, value in enumerate(conv(inp, at, wm1, 4)):
            pre[at + j] = value
            hid[at + j] = (value * jax.nn.sigmoid(value) * keep).astype(BF16)

    def second(at):
        keep = keep_of(top - 12 + at)
        for j, value in enumerate(conv(hid, at, wm2, 8)):
            sec[at + j] = (jax.nn.sigmoid(value) * keep).astype(BF16)

    def third(at):
        keep = keep_of(top - 4 + at)
        for j, value in enumerate(conv(sec, at, wm3, 8)):
            p = pre[at + j + 16]
            s = jax.nn.sigmoid(p)
            gpre[at + j] = (value * s * (1.0 + p * (1.0 - s)) * keep).astype(BF16)

    owned = ((lane >= margin) & (lane < margin + own_cols)).astype(F32)

    def fourth(at):
        result = jnp.dot(wm4[...], gathered(gpre, at, 4), preferred_element_type=F32)
        result = result[0:8] + result[8:16] + result[16:24]
        for j in range(GROUP):
            one = result[:, j * LANES : (j + 1) * LANES]
            line = (
                one[1:2]
                + pltpu.roll(one, 4, 1)[0:1]
                + pltpu.roll(one, LANES - 4, 1)[2:3]
            )
            gown[at + j : at + j + 1, :] = line * owned

    def groups(*work):
        for side in range(2):
            @pl.when(par == side)
            def _(side=side):
                for fn, count, which in work:
                    for g in which:
                        fn(count - GROUP - GROUP * g if side else GROUP * g)

    def stage(ones, twos=(), threes=(), fours=()):
        groups(
            (first, rows + 40, ones), (second, rows + 24, twos),
            (third, rows + 8, threes), (fourth, rows, fours),
        )

    each(1, tiles, lambda s: entry_arrival(s).wait_recv())
    unless_mine(
        lambda mine: entry_copy(0, True).wait() if mine else entry_arrival(0).wait_recv()
    )

    per_tile = rows // TILE_ROWS
    n_tiles = tile_hot.shape[0]
    lane_of = lax.broadcasted_iota(jnp.int32, (1, LANES), 1)
    block_q = min(to_cell.shape[1], 4 * LANES)

    def cells_of(g):
        known = [erecv[g * per + n, cap:, :].astype(F32) for n in range(per)]
        meta = known[0]
        for k in known[1:]:
            meta = meta + k
        net_row = meta[0:1, :] + (lane_of // cap * SPREAD).astype(F32)
        mine = meta[1:2, :].astype(jnp.int32)
        across = mine % per_row - wc * (own_cols // TILE_COLS)
        which = across * per_tile + mine // per_row
        which = jnp.where((across >= 0) & (across < own_cols // TILE_COLS), which, -1)
        at_g = pl.multiple_of(g * LANES, LANES)
        tile_hot[:, pl.ds(at_g, LANES)] = jnp.where(
            lax.broadcasted_iota(jnp.int32, (n_tiles, LANES), 0) == which, 1.0, 0.0
        )
        count = pins // LANES

        def pin_row(n, at):
            return jnp.concatenate([known[n][2 + at + m : 3 + at + m, :] for m in range(count)], axis=1)

        net_pin = jnp.concatenate([pin_row(n, 0) + float(n * SPREAD) for n in range(per)], axis=1)
        cell_row = jnp.concatenate(
            [pin_row(n, count) * float(LANES) + pin_row(n, 2 * count) for n in range(per)], axis=1
        )
        net_col = jnp.transpose(jnp.broadcast_to(net_row, (8, LANES)))[:, 0:1]
        same = jnp.where(net_col == net_pin, 1.0, 0.0).astype(BF16)

        def some(q):
            at_q = pl.multiple_of(q * block_q, LANES)
            number = (lax.broadcasted_iota(jnp.int32, (block_q, per * pins), 0) + q * block_q).astype(F32)
            hot = jnp.where(number == cell_row, 1.0, 0.0).astype(BF16)
            to_cell[pl.ds(at_g, LANES), pl.ds(at_q, block_q)] = lax.dot_general(
                same, hot, (((1,), (1,)), ((), ())), preferred_element_type=F32
            ).astype(BF16)

        loop(to_cell.shape[1] // block_q, some)

    def loop(count, fn):
        if count <= 4:
            for n in range(count):
                fn(n)
        else:
            def body(n, carry):
                fn(n)
                return carry
            lax.fori_loop(0, count, body, 0)

    loop(tiles // per, cells_of)

    rim_wait("B0")
    rim_wait("B1")
    stage(range(6, 12))
    rim_wait("A0")
    rim_start("R")
    stage(range(4, 6))
    rim_wait("R")
    stage(range(12, 14), range(4, 10), range(4, 6))
    rim_wait("A1")
    stage(range(2, 4), range(2, 4), range(2, 4), range(2, 4))
    rim_wait("F")
    stage(range(0, 2), range(0, 2), range(0, 2), range(0, 2))

    grads = gown[...]
    right = lax.broadcasted_iota(jnp.int32, (TILE_ROWS, LANES), 0) == (
        lax.broadcasted_iota(jnp.int32, (TILE_ROWS, LANES), 1) // TILE_COLS
    )
    leaning = [
        pltpu.roll(
            grads[a * TILE_ROWS : (a + 1) * TILE_ROWS], 0, 1, stride=TILE_COLS, stride_axis=0
        )
        for a in range(per_tile)
    ]
    parts = []
    for b in range(own_cols // TILE_COLS):
        for a in range(per_tile):
            moved = pltpu.roll(leaning[a], (-margin - b * TILE_COLS) % LANES, 1)
            parts.append(jnp.sum(jnp.where(right, moved, 0.0), axis=0, keepdims=True))
    by_tile = jnp.concatenate(
        [p.astype(F32) for p in split(jnp.concatenate(parts, axis=0), 3)], axis=0
    ).astype(BF16)
    all_frac = erecv[:, :cap, :].reshape(tiles * cap, LANES)
    found = lax.dot_general(
        by_tile, all_frac, (((1,), (1,)), ((), ())), preferred_element_type=F32
    )
    found = found[:n_tiles] + found[n_tiles : 2 * n_tiles] + found[2 * n_tiles :]
    entry_grad = jnp.sum(found * tile_hot[...], axis=0, keepdims=True)
    pieces = jnp.concatenate(
        [p.astype(F32) for p in split(entry_grad, 3)] + [jnp.zeros((5, tiles * cap), F32)], axis=0
    ).astype(BF16)
    cells = jnp.dot(pieces, to_cell[...], preferred_element_type=F32)
    cells = cells[0:1] + cells[1:2] + cells[2:3]
    for u in range(csend.shape[0]):
        csend[u] = cells[:, u * LANES : (u + 1) * LANES]

    share = LANES // CELL_DEV

    def cell_copy(step, to):
        return pltpu.make_async_remote_copy(
            src_ref=csend.at[to[0] // share], dst_ref=crecv.at[step],
            send_sem=csend_sem, recv_sem=crecv_sem,
            device_id=to, device_id_type=MESH,
        )

    each_peer(lambda n, who: cell_copy(n, who).start())

    for q in range(2):
        for turn in range(chans):
            if turn:
                feat_copy(turn, q).wait_send()
            else:
                @pl.when(jnp.logical_not(alike))
                def _(q=q):
                    feat_copy(0, q).wait_send()
    each(1, tiles, lambda s: entry_copy(s).wait_send())

    @pl.when(jnp.logical_not(alike))
    def _():
        entry_copy(0).wait_send()

    for role in RIMS:
        rim_sent(role)
    arrived = crecv.at[pl.ds(1, others)]
    pltpu.make_async_remote_copy(
        src_ref=arrived, dst_ref=arrived, send_sem=csend_sem, recv_sem=crecv_sem,
        device_id=(ti, wrap(ci + 1, chans)), device_id_type=MESH,
    ).wait()
    total = csend[ti // share] + jnp.sum(crecv[1:], axis=0)
    for n in range(1, share):
        total = jnp.where(ti % share == n, pltpu.roll(total, LANES - n * CELL_DEV, 1), total)
    out[...] = total


def solution(mesh):
    tiles, chans = mesh.shape["tile"], mesh.shape["chan"]

    def local(
        feat, lift, w4, w8, frac, target, owner, net_e, weight, net_p, cell,
    ):
        rows, chan_own, cols = feat.shape
        chan = chan_own * chans
        entries = frac.shape[0]
        pins = weight.shape[0]
        in_rows = rows + 2 * HALO
        height = rows * tiles
        cap = -(-(2 * entries // tiles) // META) * META
        n_tiles = rows // TILE_ROWS * (cols // chans // TILE_COLS)
        vm = pltpu.VMEM
        dma = pltpu.SemaphoreType.DMA
        result = pl.pallas_call(
            functools.partial(kernel, tiles, chans),
            out_shape=jax.ShapeDtypeStruct((1, LANES), F32),
            in_specs=[pl.BlockSpec(memory_space=pltpu.HBM)] * 11,
            out_specs=pl.BlockSpec(memory_space=pltpu.VMEM),
            scratch_shapes=[
                vm(feat.shape, BF16),
                vm((1, chan), F32),
                vm(w4.shape, BF16),
                vm(w8.shape, BF16),
                vm(frac.shape, BF16),
                vm((1, entries), jnp.int32),
                vm((1, entries), jnp.int32),
                vm((1, entries), jnp.int32),
                vm((1, pins), F32),
                vm((1, pins), jnp.int32),
                vm((1, pins), jnp.int32),
                dma((11,)),
                vm((chans, rows, chan_own, LANES), BF16),
                vm((rows, chan, LANES), BF16),
                vm((in_rows, chan, LANES), BF16),
                vm((rows + 40, chan, LANES), F32),
                vm((rows + 40, chan, LANES), BF16),
                vm((rows + 24, chan, LANES), BF16),
                vm((rows + 8, chan, LANES), BF16),
                vm((3 * chan, 3 * chan), BF16),
                vm((3 * chan, 3 * chan), BF16),
                vm((3 * chan, 3 * chan), BF16),
                vm((32, 3 * chan), BF16),
                vm((entries, TILE_ROWS * LANES), BF16),
                vm((height, LANES), F32),
                vm((height, LANES), BF16),
                vm((tiles, rows, LANES), BF16),
                vm((rows, LANES), F32),
                vm((rows, LANES), F32),
                vm((tiles, cap + META, LANES), BF16),
                vm((tiles, cap + META, LANES), BF16),
                vm((tiles * cap, tiles * CELL_DEV), BF16),
                vm((n_tiles, tiles * cap), F32),
                vm((tiles * CELL_DEV // LANES, 1, LANES), F32),
                vm((tiles * chans, 1, LANES), F32),
                dma((2, chans)),
                dma((2, chans)),
                dma((4,)),
                dma((len(RIMS),)),
                dma((len(RIMS),)),
                dma((tiles,)),
                dma((tiles,)),
                dma((tiles,)),
                dma((tiles,)),
                dma(()),
                dma(()),
            ],
            compiler_params=pltpu.CompilerParams(collective_id=0, has_side_effects=True),
        )(
            feat, lift.reshape(1, chan), w4, w8, frac, target.reshape(1, entries),
            owner.reshape(1, entries), net_e.reshape(1, entries), weight.reshape(1, pins),
            net_p.reshape(1, pins), cell.reshape(1, pins),
        )
        return result[0, :CELL_DEV]

    in_specs = (
        P("tile", "chan", None), P(), P(), P(),
        P("tile", None), P("tile", None),
        P("tile"), P("tile"), P("tile"), P("tile"), P("tile"),
    )
    return jax.shard_map(
        local, mesh=mesh, in_specs=in_specs, out_specs=P("tile"), check_vma=False
    )
```

time: 36 us -> 27.4 us (0.76)
  Pallas kernels: 34.7 us -> 26.1 us
    pallas_call x1, Pallas kernels: 34.7 us -> 26.1 us  [local(): pl.pallas_call(functools.partial(kernel, tiles, chans), out_shape=jax.Sha...]
where the time goes in v1:
time: 27.4 us; the launch traced here: 27.3 us
  Pallas kernels  26.1 us (95%)
  local copies, waits for them, and re-layouts  1.19 us (4%)
    pallas_call x1, Pallas kernels, local(): pl.pallas_call(functools.partial(kernel, tiles, chans), out_shape=jax.Sha...  26.1 us
    squeeze x1, local copies, waits for them, and re-layouts, local(): return result[0, :CELL_DEV]  1.19 us

profile of v1, /device:TPU:0, one launch (start us, length us, event | category | flops | bytes accessed | tf_op | source)
XLA Modules:
  0.0 27.3 jit_solution(12817299251556457739)
XLA Ops:
  0.0 26.1 %shard_map.109 = f32[1,128]{1,0:T(1,128)} custom-call(bf16[16,16,256]{2,1,0:T(8,128)(2,1)} %feat_in.1, f32[1,64]{1,0:T(1,128)} %bitcast.15, bf16[3,3,64,64]{3,2,1,0:T(8,128)(2,1)} %w4_in.1, bf16[3,3,64,64]{3,2,1,0:T(8,128)(2,1)} %w8_in.1, bf16[256,128]{1,0:T(8,128)(2,1)} %frac_in.1, s32[1,256]{1,0:T(1,128)} %bitcast.9, s32[1,256]{1,0:T(1,128)} %bitcast.10, ...), custom_call_target="tpu_custom_call" | custom-call | tf_op jit(solution)/shard_map/pallas_call | solution.py:649
  26.1 1.2 %slice_bitcast_fusion = f32[64]{0:T(128)} fusion(f32[1,128]{1,0:T(1,128)} %shard_map.109), kind=kLoop, calls=%fused_computation | loop fusion | bytes 512 | tf_op jit(solution)/shard_map/squeeze | solution.py:708

commit v2 on v1

--- a/solution.py
+++ b/solution.py
@@ -17,6 +17,8 @@
 META = 16
 SPREAD = 4096
 RIMS = ("A0", "B0", "F", "A1", "B1", "R")
+FEAT, DEMAND, ENTRY, RIM, CELL = range(5)
+PART = 256
 F32 = jnp.float32
 BF16 = jnp.bfloat16
 
@@ -35,11 +37,10 @@
     feat_in, lift_in, w4_in, w8_in, frac_in, target_in, owner_in, net_e_in, weight_in, net_p_in,
     cell_in,
     out,
-    feat, lift, w4, w8, frac, target, owner, net_e, weight, net_p, cell, load_sem,
+    feat, lift, w4, w8, frac, numbers, weight, load_sem,
     win, gath, inp, pre, hid, sec, gpre, wm1, wm2, wm3, wm4,
     fmask, dbuf, dsend, drecv, demand, gown, esend, erecv, to_cell, tile_hot, csend, crecv,
-    fsend_sem, frecv_sem, own_sem, hsend_sem, hrecv_sem, dsend_sem, drecv_sem,
-    esend_sem, erecv_sem, csend_sem, crecv_sem,
+    send_sem, frecv_sem, hrecv_sem, drecv_sem, erecv_sem, crecv_sem,
 ):
     ti = lax.axis_index("tile")
     ci = lax.axis_index("chan")
@@ -65,18 +66,23 @@
     def at_work(t, c):
         return (t - t % 2 + c % 2, c - c % 2 + t % 2)
 
+    target, owner, net_e, net_p, cell = (numbers.at[n] for n in range(5))
     loads = [
         pltpu.make_async_copy(src, dst, load_sem.at[n])
         for n, (src, dst) in enumerate(
             [
-                (feat_in, feat), (target_in, target), (owner_in, owner), (net_e_in, net_e),
-                (weight_in, weight), (net_p_in, net_p), (frac_in, frac), (lift_in, lift),
-                (cell_in, cell), (w4_in, w4), (w8_in, w8),
+                (feat_in, feat), (weight_in, weight), (frac_in, frac), (lift_in, lift),
+                (w4_in, w4), (w8_in, w8),
             ]
         )
     ]
     for load in loads:
         load.start()
+    for src, dst in (
+        (target_in, target), (owner_in, owner), (net_e_in, net_e), (net_p_in, net_p),
+        (cell_in, cell),
+    ):
+        pltpu.make_async_copy(src, dst, load_sem.at[len(loads)]).start()
 
     barrier = pltpu.get_barrier_semaphore()
 
@@ -132,6 +138,7 @@
 
     for load in loads[1:]:
         load.wait()
+    pltpu.make_async_copy(numbers, numbers, load_sem.at[len(loads)]).wait()
     per_row = cols // TILE_COLS
     own, cell_no = owner[...], cell[...]
     target_row = target[...].astype(F32)
@@ -206,22 +213,16 @@
             pl.ds(h * half, half), pl.ds(pl.multiple_of(ci * chan_own, chan_own), chan_own)
         ]
         if mine:
-            return pltpu.make_async_copy(src, dst, own_sem.at[q])
+            return pltpu.make_async_copy(src, dst, frecv_sem.at[q])
         return pltpu.make_async_remote_copy(
             src_ref=src, dst_ref=dst,
-            send_sem=fsend_sem.at[q, turn], recv_sem=frecv_sem.at[q, turn],
+            send_sem=send_sem.at[FEAT], recv_sem=frecv_sem.at[q],
             device_id=at_work(ti, to), device_id_type=MESH,
         )
 
-    def feat_arrival(turn, q):
-        h = par if q == 0 else 1 - par
-        come = wrap(wc + chans - turn, chans)
-        dst = gath.at[
-            pl.ds(h * half, half), pl.ds(pl.multiple_of(come * chan_own, chan_own), chan_own)
-        ]
+    def came(dst, sem, n):
         return pltpu.make_async_remote_copy(
-            src_ref=dst, dst_ref=dst,
-            send_sem=fsend_sem.at[q, turn], recv_sem=frecv_sem.at[q, turn],
+            src_ref=dst, dst_ref=dst, send_sem=send_sem.at[n], recv_sem=sem,
             device_id=(ti, wrap(ci + 1, chans)), device_id_type=MESH,
         )
 
@@ -241,42 +242,28 @@
             unless_mine(lambda mine: feat_copy(0, q, mine).start())
 
     def feat_wait(q):
-        for turn in range(chans):
-            if turn:
-                feat_arrival(turn, q).wait_recv()
-            else:
-                unless_mine(
-                    lambda mine: feat_copy(0, q, True).wait()
-                    if mine else feat_arrival(0, q).wait_recv()
-                )
+        h = par if q == 0 else 1 - par
+        came(gath.at[pl.ds(h * half, half)], frecv_sem.at[q], FEAT).wait_recv()
 
     def demand_copy(step, mine=False):
         to = wrap(ti + step, tiles)
         src = dsend.at[pl.ds(pl.multiple_of(to * rows, rows), rows)]
         if mine:
-            return pltpu.make_async_copy(src, drecv.at[step], own_sem.at[2])
+            return pltpu.make_async_copy(src, drecv.at[step], drecv_sem)
         return pltpu.make_async_remote_copy(
             src_ref=src, dst_ref=drecv.at[step],
-            send_sem=dsend_sem.at[step], recv_sem=drecv_sem.at[step],
+            send_sem=send_sem.at[DEMAND], recv_sem=drecv_sem,
             device_id=at_work(to, ci), device_id_type=MESH,
         )
 
     def entry_copy(step, mine=False):
         to = wrap(ti + step, tiles)
         if mine:
-            return pltpu.make_async_copy(esend.at[to], erecv.at[ti], own_sem.at[3])
+            return pltpu.make_async_copy(esend.at[to], erecv.at[ti], erecv_sem)
         return pltpu.make_async_remote_copy(
             src_ref=esend.at[to], dst_ref=erecv.at[ti],
-            send_sem=esend_sem.at[step], recv_sem=erecv_sem.at[step],
+            send_sem=send_sem.at[ENTRY], recv_sem=erecv_sem,
             device_id=at_work(to, ci), device_id_type=MESH,
-        )
-
-    def entry_arrival(step):
-        dst = erecv.at[wrap(wt + tiles - step, tiles)]
-        return pltpu.make_async_remote_copy(
-            src_ref=dst, dst_ref=dst,
-            send_sem=esend_sem.at[step], recv_sem=erecv_sem.at[step],
-            device_id=(ti, wrap(ci + 1, chans)), device_id_type=MESH,
         )
 
     pl.semaphore_wait(barrier, others)
@@ -295,7 +282,7 @@
     key = target_row * float(cap) + rank
     pin_rows = [
         row[:, n * LANES : (n + 1) * LANES]
-        for row in (table[4:5, :], (cell_no // LANES).astype(F32), (cell_no % LANES).astype(F32))
+        for row in (table[4:5, :], (cell_no // PART).astype(F32), (cell_no % PART).astype(F32))
         for n in range(pins // LANES)
     ]
     fixed = jnp.concatenate(
@@ -349,7 +336,7 @@
                 there = inside(to)
             copy = pltpu.make_async_remote_copy(
                 src_ref=inp.at[pl.ds(start, half)], dst_ref=inp.at[pl.ds(at, half)],
-                send_sem=hsend_sem.at[n], recv_sem=hrecv_sem.at[n],
+                send_sem=send_sem.at[RIM], recv_sem=hrecv_sem.at[n],
                 device_id=at_work(to, wc), device_id_type=MESH,
             )
         else:
@@ -362,12 +349,7 @@
                 "R": (wt - 2 * near, HALO - 2 * rows * near + half * par),
             }[role]
             there = inside(come)
-            dst = inp.at[pl.ds(at, half)]
-            copy = pltpu.make_async_remote_copy(
-                src_ref=dst, dst_ref=dst,
-                send_sem=hsend_sem.at[n], recv_sem=hrecv_sem.at[n],
-                device_id=(ti, wrap(ci + 1, chans)), device_id_type=MESH,
-            )
+            copy = came(inp.at[pl.ds(at, half)], hrecv_sem.at[n], RIM)
         return there, copy
 
     def rim_start(role):
@@ -377,13 +359,6 @@
         def _():
             copy.start()
 
-    def rim_sent(role):
-        there, copy = rim(role, True)
-
-        @pl.when(there)
-        def _():
-            copy.wait_send()
-
     def rim_wait(role):
         there, copy = rim(role, False)
 
@@ -391,8 +366,7 @@
         def _():
             copy.wait_recv()
 
-    each(1, tiles, lambda s: demand_copy(s).wait())
-    unless_mine(lambda mine: demand_copy(0, mine).wait())
+    came(drecv, drecv_sem, DEMAND).wait_recv()
     demand[...] = lax.fori_loop(
         1, tiles, lambda s, t: t + drecv[s].astype(F32), drecv[0].astype(F32)
     )
@@ -489,15 +463,10 @@
             (third, rows + 8, threes), (fourth, rows, fours),
         )
 
-    each(1, tiles, lambda s: entry_arrival(s).wait_recv())
-    unless_mine(
-        lambda mine: entry_copy(0, True).wait() if mine else entry_arrival(0).wait_recv()
-    )
-
     per_tile = rows // TILE_ROWS
     n_tiles = tile_hot.shape[0]
     lane_of = lax.broadcasted_iota(jnp.int32, (1, LANES), 1)
-    block_q = min(to_cell.shape[1], 4 * LANES)
+    counted = lax.broadcasted_iota(jnp.int32, (PART, LANES), 0).astype(F32).astype(BF16)
 
     def cells_of(g):
         known = [erecv[g * per + n, cap:, :].astype(F32) for n in range(per)]
@@ -519,21 +488,30 @@
             return jnp.concatenate([known[n][2 + at + m : 3 + at + m, :] for m in range(count)], axis=1)
 
         net_pin = jnp.concatenate([pin_row(n, 0) + float(n * SPREAD) for n in range(per)], axis=1)
-        cell_row = jnp.concatenate(
-            [pin_row(n, count) * float(LANES) + pin_row(n, 2 * count) for n in range(per)], axis=1
-        )
+        cell_part = jnp.concatenate([pin_row(n, count) for n in range(per)], axis=1)
+        cell_row = jnp.concatenate([pin_row(n, 2 * count) for n in range(per)], axis=1)
         net_col = jnp.transpose(jnp.broadcast_to(net_row, (8, LANES)))[:, 0:1]
         same = jnp.where(net_col == net_pin, 1.0, 0.0).astype(BF16)
 
         def some(q):
-            at_q = pl.multiple_of(q * block_q, LANES)
-            number = (lax.broadcasted_iota(jnp.int32, (block_q, per * pins), 0) + q * block_q).astype(F32)
-            hot = jnp.where(number == cell_row, 1.0, 0.0).astype(BF16)
-            to_cell[pl.ds(at_g, LANES), pl.ds(at_q, block_q)] = lax.dot_general(
+            at_q = pl.multiple_of(q * PART, PART)
+            part = jnp.asarray(q, F32) if isinstance(q, int) else q.astype(F32)
+            row = jnp.where(cell_part == part, cell_row, -1.0)
+            hot = jnp.concatenate(
+                [
+                    jnp.where(
+                        counted == row[:, n * LANES : (n + 1) * LANES].astype(BF16),
+                        jnp.ones((), BF16), jnp.zeros((), BF16),
+                    )
+                    for n in range(row.shape[1] // LANES)
+                ],
+                axis=1,
+            )
+            to_cell[pl.ds(at_g, LANES), pl.ds(at_q, PART)] = lax.dot_general(
                 same, hot, (((1,), (1,)), ((), ())), preferred_element_type=F32
             ).astype(BF16)
 
-        loop(to_cell.shape[1] // block_q, some)
+        loop(to_cell.shape[1] // PART, some)
 
     def loop(count, fn):
         if count <= 4:
@@ -545,20 +523,19 @@
                 return carry
             lax.fori_loop(0, count, body, 0)
 
-    loop(tiles // per, cells_of)
-
     rim_wait("B0")
     rim_wait("B1")
     stage(range(6, 12))
     rim_wait("A0")
     rim_start("R")
     stage(range(4, 6))
+    came(erecv, erecv_sem, ENTRY).wait_recv()
+    loop(tiles // per, cells_of)
     rim_wait("R")
     stage(range(12, 14), range(4, 10), range(4, 6))
     rim_wait("A1")
-    stage(range(2, 4), range(2, 4), range(2, 4), range(2, 4))
     rim_wait("F")
-    stage(range(0, 2), range(0, 2), range(0, 2), range(0, 2))
+    stage(range(0, 4), range(0, 4), range(0, 4), range(0, 4))
 
     grads = gown[...]
     right = lax.broadcasted_iota(jnp.int32, (TILE_ROWS, LANES), 0) == (
@@ -597,33 +574,28 @@
     def cell_copy(step, to):
         return pltpu.make_async_remote_copy(
             src_ref=csend.at[to[0] // share], dst_ref=crecv.at[step],
-            send_sem=csend_sem, recv_sem=crecv_sem,
+            send_sem=send_sem.at[CELL], recv_sem=crecv_sem,
             device_id=to, device_id_type=MESH,
         )
 
     each_peer(lambda n, who: cell_copy(n, who).start())
 
-    for q in range(2):
-        for turn in range(chans):
-            if turn:
-                feat_copy(turn, q).wait_send()
-            else:
-                @pl.when(jnp.logical_not(alike))
-                def _(q=q):
-                    feat_copy(0, q).wait_send()
-    each(1, tiles, lambda s: entry_copy(s).wait_send())
-
-    @pl.when(jnp.logical_not(alike))
-    def _():
-        entry_copy(0).wait_send()
-
-    for role in RIMS:
-        rim_sent(role)
+    def sent(n, ref):
+        came(ref, crecv_sem, n).wait_send()
+
+    unless_mine(lambda mine: sent(FEAT, win.at[pl.ds(0, chans - mine)]))
+    unless_mine(lambda mine: sent(DEMAND, dsend.at[pl.ds(0, (tiles - mine) * rows)]))
+    unless_mine(lambda mine: sent(ENTRY, esend.at[pl.ds(0, tiles - mine)]))
+    ahead, behind = inside(wt + near), inside(wt - 2 * near)
+    for there, count in (
+        (ahead & behind, 6), (ahead & jnp.logical_not(behind), 5),
+        (jnp.logical_not(ahead) & behind, 3), (jnp.logical_not(ahead | behind), 2),
+    ):
+        @pl.when(there)
+        def _(count=count):
+            sent(RIM, inp.at[pl.ds(0, count * half)])
     arrived = crecv.at[pl.ds(1, others)]
-    pltpu.make_async_remote_copy(
-        src_ref=arrived, dst_ref=arrived, send_sem=csend_sem, recv_sem=crecv_sem,
-        device_id=(ti, wrap(ci + 1, chans)), device_id_type=MESH,
-    ).wait()
+    came(arrived, crecv_sem, CELL).wait()
     total = csend[ti // share] + jnp.sum(crecv[1:], axis=0)
     for n in range(1, share):
         total = jnp.where(ti % share == n, pltpu.roll(total, LANES - n * CELL_DEV, 1), total)
@@ -648,7 +620,7 @@
         dma = pltpu.SemaphoreType.DMA
         result = pl.pallas_call(
             functools.partial(kernel, tiles, chans),
-            out_shape=jax.ShapeDtypeStruct((1, LANES), F32),
+            out_shape=pltpu.VMEM((1, LANES), F32),
             in_specs=[pl.BlockSpec(memory_space=pltpu.HBM)] * 11,
             out_specs=pl.BlockSpec(memory_space=pltpu.VMEM),
             scratch_shapes=[
@@ -657,13 +629,9 @@
                 vm(w4.shape, BF16),
                 vm(w8.shape, BF16),
                 vm(frac.shape, BF16),
-                vm((1, entries), jnp.int32),
-                vm((1, entries), jnp.int32),
-                vm((1, entries), jnp.int32),
+                vm((5, 1, entries), jnp.int32),
                 vm((1, pins), F32),
-                vm((1, pins), jnp.int32),
-                vm((1, pins), jnp.int32),
-                dma((11,)),
+                dma((7,)),
                 vm((chans, rows, chan_own, LANES), BF16),
                 vm((rows, chan, LANES), BF16),
                 vm((in_rows, chan, LANES), BF16),
@@ -687,15 +655,10 @@
                 vm((n_tiles, tiles * cap), F32),
                 vm((tiles * CELL_DEV // LANES, 1, LANES), F32),
                 vm((tiles * chans, 1, LANES), F32),
-                dma((2, chans)),
-                dma((2, chans)),
-                dma((4,)),
+                dma((5,)),
+                dma((2,)),
                 dma((len(RIMS),)),
-                dma((len(RIMS),)),
-                dma((tiles,)),
-                dma((tiles,)),
-                dma((tiles,)),
-                dma((tiles,)),
+                dma(()),
                 dma(()),
                 dma(()),
             ],

time: 27.4 us -> 25.6 us (0.934)
  Pallas kernels: 26.1 us -> 24.9 us
  local copies, waits for them, and re-layouts: 1.19 us -> 0.51 us
    pallas_call x1, Pallas kernels: 26.1 us -> 24.9 us  [local(): pl.pallas_call(functools.partial(kernel, tiles, chans), out_shape=pltpu.V...]
    squeeze x1, local copies, waits for them, and re-layouts: 1.19 us -> 0.51 us  [local(): return result[0, :CELL_DEV]]
where the time goes in v2:
time: 25.6 us; the launch traced here: 25.4 us
  Pallas kernels  24.9 us (97%)
  local copies, waits for them, and re-layouts  0.51 us (2%)
    pallas_call x1, Pallas kernels, local(): pl.pallas_call(functools.partial(kernel, tiles, chans), out_shape=pltpu.V...  24.9 us
    squeeze x1, local copies, waits for them, and re-layouts, local(): return result[0, :CELL_DEV]  0.51 us

profile of v2, /device:TPU:0, one launch (start us, length us, event | category | flops | bytes accessed | tf_op | source)
XLA Modules:
  0.0 25.4 jit_solution(5797882514046148616)
XLA Ops:
  0.0 24.9 %shard_map.109 = f32[1,128]{1,0:T(1,128)S(1)} custom-call(bf16[16,16,256]{2,1,0:T(8,128)(2,1)} %feat_in.1, f32[1,64]{1,0:T(1,128)} %bitcast.15, bf16[3,3,64,64]{3,2,1,0:T(8,128)(2,1)} %w4_in.1, bf16[3,3,64,64]{3,2,1,0:T(8,128)(2,1)} %w8_in.1, bf16[256,128]{1,0:T(8,128)(2,1)} %frac_in.1, s32[1,256]{1,0:T(1,128)} %bitcast.9, s32[1,256]{1,0:T(1,128)} %bitcast.10, ...), custom_call_target="tpu_custom_call" | custom-call | tf_op jit(solution)/shard_map/pallas_call | solution.py:621
  24.9 0.5 %slice_bitcast_fusion = f32[64]{0:T(128)} fusion(f32[1,128]{1,0:T(1,128)S(1)} %shard_map.109), kind=kLoop, calls=%fused_computation | loop fusion | bytes 512 | tf_op jit(solution)/shard_map/squeeze | solution.py:671

commit v3 on v2

--- a/solution.py
+++ b/solution.py
@@ -14,7 +14,7 @@
 LANES = 128
 HALO = 24
 GROUP = 4
-META = 16
+META = 8
 SPREAD = 4096
 RIMS = ("A0", "B0", "F", "A1", "B1", "R")
 FEAT, DEMAND, ENTRY, RIM, CELL = range(5)
@@ -178,6 +178,74 @@
         dbuf[pl.ds(i, blocks, stride=TILE_ROWS), :] = partial[:, i * LANES : (i + 1) * LANES]
     dsend[...] = dbuf[...].astype(BF16)
 
+    def feat_copy(turn, q, mine=False):
+        h = ti % 2 if q == 0 else 1 - ti % 2
+        to = wrap(ci + turn, chans)
+        src = win.at[to, pl.ds(h * half, half)]
+        dst = gath.at[
+            pl.ds(h * half, half), pl.ds(pl.multiple_of(ci * chan_own, chan_own), chan_own)
+        ]
+        if mine:
+            return pltpu.make_async_copy(src, dst, frecv_sem.at[q])
+        return pltpu.make_async_remote_copy(
+            src_ref=src, dst_ref=dst,
+            send_sem=send_sem.at[FEAT], recv_sem=frecv_sem.at[q],
+            device_id=at_work(ti, to), device_id_type=MESH,
+        )
+
+    def came(dst, sem, n):
+        return pltpu.make_async_remote_copy(
+            src_ref=dst, dst_ref=dst, send_sem=send_sem.at[n], recv_sem=sem,
+            device_id=(ti, wrap(ci + 1, chans)), device_id_type=MESH,
+        )
+
+    def unless_mine(fn):
+        @pl.when(jnp.logical_not(alike))
+        def _():
+            fn(False)
+
+        @pl.when(alike)
+        def _():
+            fn(True)
+
+    def feat_send(turn, q):
+        if turn:
+            feat_copy(turn, q).start()
+        else:
+            unless_mine(lambda mine: feat_copy(0, q, mine).start())
+
+    def feat_wait(q):
+        h = par if q == 0 else 1 - par
+        came(gath.at[pl.ds(h * half, half)], frecv_sem.at[q], FEAT).wait_recv()
+
+    def demand_copy(step, mine=False):
+        to = wrap(ti + step, tiles)
+        src = dsend.at[pl.ds(pl.multiple_of(to * rows, rows), rows)]
+        if mine:
+            return pltpu.make_async_copy(src, drecv.at[step], drecv_sem)
+        return pltpu.make_async_remote_copy(
+            src_ref=src, dst_ref=drecv.at[step],
+            send_sem=send_sem.at[DEMAND], recv_sem=drecv_sem,
+            device_id=at_work(to, ci), device_id_type=MESH,
+        )
+
+    def entry_copy(step, mine=False):
+        to = wrap(ti + step, tiles)
+        if mine:
+            return pltpu.make_async_copy(esend.at[to], erecv.at[ti], erecv_sem)
+        return pltpu.make_async_remote_copy(
+            src_ref=esend.at[to], dst_ref=erecv.at[ti],
+            send_sem=send_sem.at[ENTRY], recv_sem=erecv_sem,
+            device_id=at_work(to, ci), device_id_type=MESH,
+        )
+
+    pl.semaphore_wait(barrier, others)
+    each(1, tiles, lambda s: demand_copy(s).start())
+    unless_mine(lambda mine: demand_copy(0, mine).start())
+    for q in range(2):
+        for turn in range(chans - 1, -1, -1):
+            feat_send(turn, q)
+
     lift_row = lift[...]
     lift_col = jnp.transpose(jnp.broadcast_to(lift_row, (LANES, chan)))
     for u in range(3):
@@ -205,74 +273,6 @@
         [hi, mid, low_part, jnp.zeros((8, 3 * chan), F32)], axis=0
     ).astype(BF16)
 
-    def feat_copy(turn, q, mine=False):
-        h = ti % 2 if q == 0 else 1 - ti % 2
-        to = wrap(ci + turn, chans)
-        src = win.at[to, pl.ds(h * half, half)]
-        dst = gath.at[
-            pl.ds(h * half, half), pl.ds(pl.multiple_of(ci * chan_own, chan_own), chan_own)
-        ]
-        if mine:
-            return pltpu.make_async_copy(src, dst, frecv_sem.at[q])
-        return pltpu.make_async_remote_copy(
-            src_ref=src, dst_ref=dst,
-            send_sem=send_sem.at[FEAT], recv_sem=frecv_sem.at[q],
-            device_id=at_work(ti, to), device_id_type=MESH,
-        )
-
-    def came(dst, sem, n):
-        return pltpu.make_async_remote_copy(
-            src_ref=dst, dst_ref=dst, send_sem=send_sem.at[n], recv_sem=sem,
-            device_id=(ti, wrap(ci + 1, chans)), device_id_type=MESH,
-        )
-
-    def unless_mine(fn):
-        @pl.when(jnp.logical_not(alike))
-        def _():
-            fn(False)
-
-        @pl.when(alike)
-        def _():
-            fn(True)
-
-    def feat_send(turn, q):
-        if turn:
-            feat_copy(turn, q).start()
-        else:
-            unless_mine(lambda mine: feat_copy(0, q, mine).start())
-
-    def feat_wait(q):
-        h = par if q == 0 else 1 - par
-        came(gath.at[pl.ds(h * half, half)], frecv_sem.at[q], FEAT).wait_recv()
-
-    def demand_copy(step, mine=False):
-        to = wrap(ti + step, tiles)
-        src = dsend.at[pl.ds(pl.multiple_of(to * rows, rows), rows)]
-        if mine:
-            return pltpu.make_async_copy(src, drecv.at[step], drecv_sem)
-        return pltpu.make_async_remote_copy(
-            src_ref=src, dst_ref=drecv.at[step],
-            send_sem=send_sem.at[DEMAND], recv_sem=drecv_sem,
-            device_id=at_work(to, ci), device_id_type=MESH,
-        )
-
-    def entry_copy(step, mine=False):
-        to = wrap(ti + step, tiles)
-        if mine:
-            return pltpu.make_async_copy(esend.at[to], erecv.at[ti], erecv_sem)
-        return pltpu.make_async_remote_copy(
-            src_ref=esend.at[to], dst_ref=erecv.at[ti],
-            send_sem=send_sem.at[ENTRY], recv_sem=erecv_sem,
-            device_id=at_work(to, ci), device_id_type=MESH,
-        )
-
-    pl.semaphore_wait(barrier, others)
-    each(1, tiles, lambda s: demand_copy(s).start())
-    unless_mine(lambda mine: demand_copy(0, mine).start())
-    for q in range(2):
-        for turn in range(chans - 1, -1, -1):
-            feat_send(turn, q)
-
     before = lax.broadcasted_iota(jnp.int32, (entries, entries), 0) < lax.broadcasted_iota(
         jnp.int32, (entries, entries), 1
     )
@@ -287,7 +287,7 @@
     ]
     fixed = jnp.concatenate(
         [jnp.zeros((2, LANES), F32)] + pin_rows
-        + [jnp.zeros((META - 2 - len(pin_rows), LANES), F32)],
+        + [jnp.zeros((1, LANES), F32)] * (META - 2 - len(pin_rows)),
         axis=0,
     )
     loose = jnp.concatenate(
@@ -383,7 +383,6 @@
     rim_start("B0")
     feat_wait(1)
     fill(1 - par)
-    rim_start("F")
     rim_start("A1")
     rim_start("B1")
 
@@ -525,12 +524,13 @@
 
     rim_wait("B0")
     rim_wait("B1")
+    rim_start("F")
     stage(range(6, 12))
+    came(erecv, erecv_sem, ENTRY).wait_recv()
+    loop(tiles // per, cells_of)
     rim_wait("A0")
     rim_start("R")
     stage(range(4, 6))
-    came(erecv, erecv_sem, ENTRY).wait_recv()
-    loop(tiles // per, cells_of)
     rim_wait("R")
     stage(range(12, 14), range(4, 10), range(4, 6))
     rim_wait("A1")
@@ -614,7 +614,7 @@
         pins = weight.shape[0]
         in_rows = rows + 2 * HALO
         height = rows * tiles
-        cap = -(-(2 * entries // tiles) // META) * META
+        cap = -(-(2 * entries // tiles) // 16) * 16
         n_tiles = rows // TILE_ROWS * (cols // chans // TILE_COLS)
         vm = pltpu.VMEM
         dma = pltpu.SemaphoreType.DMA

time: 25.6 us -> 24.5 us (0.957)
  Pallas kernels: 24.9 us -> 23.9 us
    pallas_call x1, Pallas kernels: 24.9 us -> 23.9 us  [local(): pl.pallas_call(functools.partial(kernel, tiles, chans), out_shape=pltpu.V...]
where the time goes in v3:
time: 24.5 us; the launch traced here: 24.4 us
  Pallas kernels  23.9 us (98%)
  local copies, waits for them, and re-layouts  0.51 us (2%)
    pallas_call x1, Pallas kernels, local(): pl.pallas_call(functools.partial(kernel, tiles, chans), out_shape=pltpu.V...  23.9 us
    squeeze x1, local copies, waits for them, and re-layouts, local(): return result[0, :CELL_DEV]  0.51 us

profile of v3, /device:TPU:0, one launch (start us, length us, event | category | flops | bytes accessed | tf_op | source)
XLA Modules:
  0.0 24.4 jit_solution(2352877510952900926)
XLA Ops:
  0.0 23.9 %shard_map.109 = f32[1,128]{1,0:T(1,128)S(1)} custom-call(bf16[16,16,256]{2,1,0:T(8,128)(2,1)} %feat_in.1, f32[1,64]{1,0:T(1,128)} %bitcast.15, bf16[3,3,64,64]{3,2,1,0:T(8,128)(2,1)} %w4_in.1, bf16[3,3,64,64]{3,2,1,0:T(8,128)(2,1)} %w8_in.1, bf16[256,128]{1,0:T(8,128)(2,1)} %frac_in.1, s32[1,256]{1,0:T(1,128)} %bitcast.9, s32[1,256]{1,0:T(1,128)} %bitcast.10, ...), custom_call_target="tpu_custom_call" | custom-call | tf_op jit(solution)/shard_map/pallas_call | solution.py:621
  23.9 0.5 %slice_bitcast_fusion = f32[64]{0:T(128)} fusion(f32[1,128]{1,0:T(1,128)S(1)} %shard_map.109), kind=kLoop, calls=%fused_computation | loop fusion | bytes 512 | tf_op jit(solution)/shard_map/squeeze | solution.py:671

commit v4 on v3

--- a/solution.py
+++ b/solution.py
@@ -19,6 +19,7 @@
 RIMS = ("A0", "B0", "F", "A1", "B1", "R")
 FEAT, DEMAND, ENTRY, RIM, CELL = range(5)
 PART = 256
+PIECES = 4
 F32 = jnp.float32
 BF16 = jnp.bfloat16
 
@@ -49,6 +50,7 @@
     own_cols = cols // chans
     margin = (LANES - own_cols) // 2
     half = rows // 2
+    some_rows = rows // PIECES
     in_rows = rows + 2 * HALO
     others = tiles * chans - 1
     entries, pins = frac.shape[0], weight.shape[1]
@@ -178,12 +180,15 @@
         dbuf[pl.ds(i, blocks, stride=TILE_ROWS), :] = partial[:, i * LANES : (i + 1) * LANES]
     dsend[...] = dbuf[...].astype(BF16)
 
+    def piece(side, q):
+        return (q + side * (PIECES - 1 - 2 * q)) * some_rows
+
     def feat_copy(turn, q, mine=False):
-        h = ti % 2 if q == 0 else 1 - ti % 2
+        low = piece(ti % 2, q)
         to = wrap(ci + turn, chans)
-        src = win.at[to, pl.ds(h * half, half)]
+        src = win.at[to, pl.ds(low, some_rows)]
         dst = gath.at[
-            pl.ds(h * half, half), pl.ds(pl.multiple_of(ci * chan_own, chan_own), chan_own)
+            pl.ds(low, some_rows), pl.ds(pl.multiple_of(ci * chan_own, chan_own), chan_own)
         ]
         if mine:
             return pltpu.make_async_copy(src, dst, frecv_sem.at[q])
@@ -215,8 +220,7 @@
             unless_mine(lambda mine: feat_copy(0, q, mine).start())
 
     def feat_wait(q):
-        h = par if q == 0 else 1 - par
-        came(gath.at[pl.ds(h * half, half)], frecv_sem.at[q], FEAT).wait_recv()
+        came(gath.at[pl.ds(piece(par, q), some_rows)], frecv_sem.at[q], FEAT).wait_recv()
 
     def demand_copy(step, mine=False):
         to = wrap(ti + step, tiles)
@@ -242,7 +246,7 @@
     pl.semaphore_wait(barrier, others)
     each(1, tiles, lambda s: demand_copy(s).start())
     unless_mine(lambda mine: demand_copy(0, mine).start())
-    for q in range(2):
+    for q in range(PIECES):
         for turn in range(chans - 1, -1, -1):
             feat_send(turn, q)
 
@@ -314,16 +318,7 @@
     unless_mine(lambda mine: entry_copy(0, mine).start())
 
     def rim(role, sending):
-        if role == "A0":
-            to, h = wt + near, par
-        elif role == "A1":
-            to, h = wt + near, 1 - par
-        elif role == "B0":
-            to, h = wt - near, par
-        elif role == "B1":
-            to, h = wt - near, 1 - par
-        else:
-            to, h = wt - 2 * near, 1 - par
+        to, h = wt - 2 * near, 1 - par
         n = RIMS.index(role)
         if sending:
             start = HALO + h * half
@@ -371,20 +366,29 @@
         1, tiles, lambda s, t: t + drecv[s].astype(F32), drecv[0].astype(F32)
     )
 
-    def fill(h):
-        for j in range(half):
-            row = h * half + j
+    def fill(q):
+        for j in range(some_rows):
+            row = piece(par, q) + j
             add = lift_col * demand[pl.ds(row, 1), :]
             inp[HALO + row] = (gath[row].astype(F32) + add).astype(BF16)
 
-    feat_wait(0)
-    fill(par)
-    rim_start("A0")
-    rim_start("B0")
-    feat_wait(1)
-    fill(1 - par)
-    rim_start("A1")
-    rim_start("B1")
+    def near_start(q):
+        low = piece(par, q)
+        n = 2 * q // PIECES
+        for role, to in (("A", wt + near), ("B", wt - near)):
+            @pl.when(inside(to))
+            def _(role=role, to=to):
+                pltpu.make_async_remote_copy(
+                    src_ref=inp.at[pl.ds(HALO + low, some_rows)],
+                    dst_ref=inp.at[pl.ds(HALO + (wt - to) * rows + low, some_rows)],
+                    send_sem=send_sem.at[RIM], recv_sem=hrecv_sem.at[RIMS.index(role + str(n))],
+                    device_id=at_work(to, wc), device_id_type=MESH,
+                ).start()
+
+    for q in range(PIECES):
+        feat_wait(q)
+        fill(q)
+        near_start(q)
 
     def in_map(row):
         return (row >= 0) & (row < height)
@@ -522,17 +526,27 @@
                 return carry
             lax.fori_loop(0, count, body, 0)
 
+
+    @pl.when(alike)
+    def _():
+        came(erecv, erecv_sem, ENTRY).wait_recv()
+        loop(tiles // per, cells_of)
+
     rim_wait("B0")
     rim_wait("B1")
     rim_start("F")
     stage(range(6, 12))
-    came(erecv, erecv_sem, ENTRY).wait_recv()
-    loop(tiles // per, cells_of)
+
+    @pl.when(jnp.logical_not(alike))
+    def _():
+        came(erecv, erecv_sem, ENTRY).wait_recv()
+        loop(tiles // per, cells_of)
+
     rim_wait("A0")
     rim_start("R")
-    stage(range(4, 6))
+    stage(range(4, 6), range(4, 8))
     rim_wait("R")
-    stage(range(12, 14), range(4, 10), range(4, 6))
+    stage(range(12, 14), range(8, 10), range(4, 6))
     rim_wait("A1")
     rim_wait("F")
     stage(range(0, 4), range(0, 4), range(0, 4), range(0, 4))
@@ -656,7 +670,7 @@
                 vm((tiles * CELL_DEV // LANES, 1, LANES), F32),
                 vm((tiles * chans, 1, LANES), F32),
                 dma((5,)),
-                dma((2,)),
+                dma((PIECES,)),
                 dma((len(RIMS),)),
                 dma(()),
                 dma(()),

time: 24.5 us -> 24.3 us (level)
  Pallas kernels: 23.9 us -> 23.6 us
    pallas_call x1, Pallas kernels: 23.9 us -> 23.6 us  [local(): pl.pallas_call(functools.partial(kernel, tiles, chans), out_shape=pltpu.V...]
where the time goes in v4:
time: 24.3 us; the launch traced here: 24.1 us
  Pallas kernels  23.6 us (97%)
  local copies, waits for them, and re-layouts  0.51 us (2%)
    pallas_call x1, Pallas kernels, local(): pl.pallas_call(functools.partial(kernel, tiles, chans), out_shape=pltpu.V...  23.6 us
    squeeze x1, local copies, waits for them, and re-layouts, local(): return result[0, :CELL_DEV]  0.51 us

profile of v4, /device:TPU:0, one launch (start us, length us, event | category | flops | bytes accessed | tf_op | source)
XLA Modules:
  0.0 24.1 jit_solution(5241464046810106060)
XLA Ops:
  0.0 23.6 %shard_map.109 = f32[1,128]{1,0:T(1,128)S(1)} custom-call(bf16[16,16,256]{2,1,0:T(8,128)(2,1)} %feat_in.1, f32[1,64]{1,0:T(1,128)} %bitcast.15, bf16[3,3,64,64]{3,2,1,0:T(8,128)(2,1)} %w4_in.1, bf16[3,3,64,64]{3,2,1,0:T(8,128)(2,1)} %w8_in.1, bf16[256,128]{1,0:T(8,128)(2,1)} %frac_in.1, s32[1,256]{1,0:T(1,128)} %bitcast.9, s32[1,256]{1,0:T(1,128)} %bitcast.10, ...), custom_call_target="tpu_custom_call" | custom-call | tf_op jit(solution)/shard_map/pallas_call | solution.py:635
  23.6 0.5 %slice_bitcast_fusion = f32[64]{0:T(128)} fusion(f32[1,128]{1,0:T(1,128)S(1)} %shard_map.109), kind=kLoop, calls=%fused_computation | loop fusion | bytes 512 | tf_op jit(solution)/shard_map/squeeze | solution.py:685

commit v5 on v4

--- a/solution.py
+++ b/solution.py
@@ -105,11 +105,10 @@
             lax.fori_loop(lo, hi, body, 0)
 
     def each_peer(fn):
-        def along(back):
-            hop = tiles - 1 - back
+        def along(hop):
             for turn in range(chans):
                 fn(hop * chans + turn, (wrap(ti + hop, tiles), wrap(ci + turn, chans)))
-        each(0, tiles - 1, along)
+        each(1, tiles, along)
         for turn in range(1, chans):
             fn(turn, (ti, wrap(ci + turn, chans)))
 

time: 24.3 us -> 24.1 us (level)
  no operation moved by 1% of the time
where the time goes in v5:
time: 24.1 us; the launch traced here: 24 us
  Pallas kernels  23.4 us (97%)
  local copies, waits for them, and re-layouts  0.51 us (2%)
    pallas_call x1, Pallas kernels, local(): pl.pallas_call(functools.partial(kernel, tiles, chans), out_shape=pltpu.V...  23.4 us
    squeeze x1, local copies, waits for them, and re-layouts, local(): return result[0, :CELL_DEV]  0.51 us

profile of v5, /device:TPU:0, one launch (start us, length us, event | category | flops | bytes accessed | tf_op | source)
XLA Modules:
  0.0 24.0 jit_solution(13629026716550858067)
XLA Ops:
  0.0 23.4 %shard_map.109 = f32[1,128]{1,0:T(1,128)S(1)} custom-call(bf16[16,16,256]{2,1,0:T(8,128)(2,1)} %feat_in.1, f32[1,64]{1,0:T(1,128)} %bitcast.15, bf16[3,3,64,64]{3,2,1,0:T(8,128)(2,1)} %w4_in.1, bf16[3,3,64,64]{3,2,1,0:T(8,128)(2,1)} %w8_in.1, bf16[256,128]{1,0:T(8,128)(2,1)} %frac_in.1, s32[1,256]{1,0:T(1,128)} %bitcast.9, s32[1,256]{1,0:T(1,128)} %bitcast.10, ...), custom_call_target="tpu_custom_call" | custom-call | tf_op jit(solution)/shard_map/pallas_call | solution.py:634
  23.5 0.5 %slice_bitcast_fusion = f32[64]{0:T(128)} fusion(f32[1,128]{1,0:T(1,128)S(1)} %shard_map.109), kind=kLoop, calls=%fused_computation | loop fusion | bytes 512 | tf_op jit(solution)/shard_map/squeeze | solution.py:684

commit v6 on v5

--- a/solution.py
+++ b/solution.py
@@ -411,8 +411,8 @@
             one = result[:, j * LANES : (j + 1) * LANES]
             parts.append(
                 one[chan : 2 * chan]
-                + pltpu.roll(one[:chan], dilation, 1)
-                + pltpu.roll(one[2 * chan :], LANES - dilation, 1)
+                + pltpu.roll(one[:chan].astype(BF16), dilation, 1).astype(F32)
+                + pltpu.roll(one[2 * chan :].astype(BF16), LANES - dilation, 1).astype(F32)
             )
         return parts
 

time: 24.1 us -> 24 us (level)
  no operation moved by 1% of the time
where the time goes in v6:
time: 24 us; the launch traced here: 23.8 us
  Pallas kernels  23.3 us (97%)
  local copies, waits for them, and re-layouts  0.51 us (2%)
    pallas_call x1, Pallas kernels, local(): pl.pallas_call(functools.partial(kernel, tiles, chans), out_shape=pltpu.V...  23.3 us
    squeeze x1, local copies, waits for them, and re-layouts, local(): return result[0, :CELL_DEV]  0.51 us

profile of v6, /device:TPU:0, one launch (start us, length us, event | category | flops | bytes accessed | tf_op | source)
XLA Modules:
  0.0 23.8 jit_solution(4128052791431399282)
XLA Ops:
  0.0 23.3 %shard_map.109 = f32[1,128]{1,0:T(1,128)S(1)} custom-call(bf16[16,16,256]{2,1,0:T(8,128)(2,1)} %feat_in.1, f32[1,64]{1,0:T(1,128)} %bitcast.15, bf16[3,3,64,64]{3,2,1,0:T(8,128)(2,1)} %w4_in.1, bf16[3,3,64,64]{3,2,1,0:T(8,128)(2,1)} %w8_in.1, bf16[256,128]{1,0:T(8,128)(2,1)} %frac_in.1, s32[1,256]{1,0:T(1,128)} %bitcast.9, s32[1,256]{1,0:T(1,128)} %bitcast.10, ...), custom_call_target="tpu_custom_call" | custom-call | tf_op jit(solution)/shard_map/pallas_call | solution.py:634
  23.3 0.5 %slice_bitcast_fusion = f32[64]{0:T(128)} fusion(f32[1,128]{1,0:T(1,128)S(1)} %shard_map.109), kind=kLoop, calls=%fused_computation | loop fusion | bytes 512 | tf_op jit(solution)/shard_map/squeeze | solution.py:684

commit v7 on v6

--- a/solution.py
+++ b/solution.py
@@ -609,7 +609,12 @@
             sent(RIM, inp.at[pl.ds(0, count * half)])
     arrived = crecv.at[pl.ds(1, others)]
     came(arrived, crecv_sem, CELL).wait()
-    total = csend[ti // share] + jnp.sum(crecv[1:], axis=0)
+    chain = -(-others // 4)
+    sums = [
+        jnp.sum(crecv[low : min(low + chain, others + 1)], axis=0)
+        for low in range(1, others + 1, chain)
+    ]
+    total = csend[ti // share] + ((sums[0] + sums[1]) + (sums[2] + sums[3]))
     for n in range(1, share):
         total = jnp.where(ti % share == n, pltpu.roll(total, LANES - n * CELL_DEV, 1), total)
     out[...] = total

time: 24 us -> 23.9 us (level)
  no operation moved by 1% of the time
where the time goes in v7:
time: 23.9 us; the launch traced here: 23.8 us
  Pallas kernels  23.3 us (97%)
  local copies, waits for them, and re-layouts  0.51 us (2%)
    pallas_call x1, Pallas kernels, local(): pl.pallas_call(functools.partial(kernel, tiles, chans), out_shape=pltpu.V...  23.3 us
    squeeze x1, local copies, waits for them, and re-layouts, local(): return result[0, :CELL_DEV]  0.51 us

profile of v7, /device:TPU:0, one launch (start us, length us, event | category | flops | bytes accessed | tf_op | source)
XLA Modules:
  0.0 23.8 jit_solution(6827240087273926950)
XLA Ops:
  0.0 23.3 %shard_map.109 = f32[1,128]{1,0:T(1,128)S(1)} custom-call(bf16[16,16,256]{2,1,0:T(8,128)(2,1)} %feat_in.1, f32[1,64]{1,0:T(1,128)} %bitcast.15, bf16[3,3,64,64]{3,2,1,0:T(8,128)(2,1)} %w4_in.1, bf16[3,3,64,64]{3,2,1,0:T(8,128)(2,1)} %w8_in.1, bf16[256,128]{1,0:T(8,128)(2,1)} %frac_in.1, s32[1,256]{1,0:T(1,128)} %bitcast.9, s32[1,256]{1,0:T(1,128)} %bitcast.10, ...), custom_call_target="tpu_custom_call" | custom-call | tf_op jit(solution)/shard_map/pallas_call | solution.py:639
  23.3 0.5 %slice_bitcast_fusion = f32[64]{0:T(128)} fusion(f32[1,128]{1,0:T(1,128)S(1)} %shard_map.109), kind=kLoop, calls=%fused_computation | loop fusion | bytes 512 | tf_op jit(solution)/shard_map/squeeze | solution.py:689
